TPU v7x, 128 devices: a whole 4x4x4 slice. The times are simulated.
128 devices in a mesh: group: 8 (over x_lo, z), tensor: 16 (over x_hi, y, core).
Axes of the slice: x: 4 (x_hi: 2, x_lo: 2; x = x_hi * 2 + x_lo), y: 4, z: 4, core: 2. Of those that a mesh axis runs over, the one named last changes fastest.
Arguments:
- hidden: bfloat16 [12288, 2048], P(('group', 'tensor')), may hold values from -20 to 20
- request_of: int32 [12288], P('group'), may hold values from 0 to 191, as said below
- positions: int32 [12288], P('group'), may hold values from 0 to 511, as said below
- page_table: int32 [8, 64], P('group'), may hold values from 0 to 63, each once within a row
- attn_gain: float32 [2048], replicated, may hold values from 0.5 to 1.5
- mlp_gain: float32 [2048], replicated, may hold values from 0.5 to 1.5
- wq: float32 [2048, 2048], P('group', 'tensor'), may hold values from -2 to 2
- wk: float32 [2048, 1024], P('group', 'tensor'), may hold values from -1 to 1
- wv: float32 [2048, 1024], P('group', 'tensor'), may hold values from -0.125 to 0.125
- wo: float32 [2048, 2048], P('tensor', 'group'), may hold values from -0.125 to 0.125
- w_gate: float32 [2048, 8192], P('group', 'tensor'), may hold values from -0.125 to 0.125
- w_up: float32 [2048, 8192], P('group', 'tensor'), may hold values from -0.125 to 0.125
- w_down: float32 [8192, 2048], P('tensor', 'group'), may hold values from -0.0625 to 0.0625
Outputs:
- layer_out: bfloat16 [12288, 2048], P(('group', 'tensor'))
- kv_pages: bfloat16 [512, 128, 2048], P('group', None, 'tensor')
Inputs may be any that keep to these rules, and one draw needn't show every extreme that they name: `request_of`: prompt numbers rise strictly along the token stream, starting at 0, and the last prompt of the stream has the number 12288 // 64 - 1; a prompt's rows are consecutive, and a prompt that reaches the last row of one block of 1536 rows continues at the first row of the next block. A prompt's rows have positions 0, 1, 2 and so on in order; a prompt has at most 512 rows, and one has exactly 512.
All inputs are finite; a program needn't handle non-finite values.
Results may differ from a plain program's by a relative error of at most 0.014.
Values may be sent and summed in bfloat16 or wider, within the bound.
A program may use at most 128 MiB of HBM per device.

v0:
```python
import jax
import jax.numpy as jnp
from jax import lax
from jax.sharding import PartitionSpec as P

QH = 16
KVH = 8
HD = 128
PAGE = 128
rope_base = 1000000.0
norm_eps = 1e-06


def partner(value, axis, distance):
    mask = 2**distance
    pairs = [(source, source ^ mask) for source in range(lax.axis_size(axis))]
    return lax.ppermute(value, axis, pairs)


def from_behind(block, axis, distance):
    devices = range(lax.axis_size(axis))
    route = [(i - distance, i) for i in devices if i - distance in devices]
    return lax.ppermute(block, axis, route)


def rms_scale(values, gain):
    square = jnp.mean(values * values, axis=-1, keepdims=True)
    return (values * lax.rsqrt(square + norm_eps) * gain).astype(jnp.bfloat16)


def rotate(values, places):
    half_dim = values.shape[-1] // 2
    frequency = rope_base ** (-(jnp.arange(half_dim, dtype=jnp.float32) * 2.0 / values.shape[-1]))
    angle = places.astype(jnp.float32)[:, None] * frequency[None, :]
    cosine = jnp.cos(angle)[:, None, :]
    sine = jnp.sin(angle)[:, None, :]
    widened = values.astype(jnp.float32)
    first = widened[..., :half_dim]
    second = widened[..., half_dim:]
    return jnp.concatenate(
        [first * cosine - second * sine, second * cosine + first * sine], axis=-1
    ).astype(jnp.bfloat16)


def join_halves(own_part, other_part):
    even = lax.axis_index("tensor") % 2 == 0
    lower = jnp.where(even, own_part, other_part)
    upper = jnp.where(even, other_part, own_part)
    return jnp.concatenate([lower, upper], axis=-1)


def contract_rows(acts, pieces):
    return tuple((jnp.dot(acts, piece, preferred_element_type=jnp.float32) for piece in pieces))


def body(
    hidden,
    request_of,
    positions,
    page_table,
    attn_gain,
    mlp_gain,
    wq,
    wk,
    wv,
    wo,
    w_gate,
    w_up,
    w_down,
):
    tensor_count = lax.axis_size("tensor")
    rows_dev = hidden.shape[0]
    tok_group = request_of.shape[0]
    query_heads = QH // tensor_count
    key_heads = max(1, KVH // tensor_count)
    group_ratio = QH // KVH
    residual = lax.all_gather(hidden, "tensor", axis=0, tiled=True).astype(jnp.float32)
    normed = rms_scale(residual, attn_gain)
    query_rows = wq.astype(jnp.bfloat16)
    key_rows = wk.astype(jnp.bfloat16)
    value_rows = wv.astype(jnp.bfloat16)
    other_key, other_value = partner((key_rows, value_rows), "tensor", 0)
    key_rows = join_halves(key_rows, other_key)
    value_rows = join_halves(value_rows, other_value)
    query_sum, key_sum, value_sum = contract_rows(
        normed,
        (
            lax.all_gather(query_rows, "group", axis=0, tiled=True),
            lax.all_gather(key_rows, "group", axis=0, tiled=True),
            lax.all_gather(value_rows, "group", axis=0, tiled=True),
        ),
    )
    query_raw = query_sum.astype(jnp.bfloat16)
    key_raw = key_sum.astype(jnp.bfloat16)
    value_raw = value_sum.astype(jnp.bfloat16)
    queries = rotate(query_raw.reshape(tok_group, query_heads, HD), positions)
    keys = rotate(key_raw.reshape(tok_group, key_heads, HD), positions)
    values = value_raw.reshape(tok_group, key_heads, HD)
    kv_rows = jnp.stack([keys, values], axis=2)
    earlier = from_behind(kv_rows, "group", 1)
    earlier_rows = earlier.shape[0]
    all_rows = jnp.concatenate([earlier, kv_rows], axis=0)
    all_keys = jnp.repeat(all_rows[:, :, 0], group_ratio, axis=1)[:, :query_heads]
    all_values = jnp.repeat(all_rows[:, :, 1], group_ratio, axis=1)[:, :query_heads]
    first_request = request_of[0]
    first_position = positions[0]
    same_local = (request_of[:, None] == request_of[None, :]) & (
        positions[None, :] <= positions[:, None]
    )
    same_earlier = (request_of[:, None] == first_request) & (
        jnp.arange(earlier_rows)[None, :] >= earlier_rows - first_position
    )
    visible = jnp.concatenate([same_earlier, same_local], axis=1)
    scores = jnp.einsum(
        "qhd,khd->hqk", queries, all_keys, preferred_element_type=jnp.float32
    ) * HD ** (-0.5)
    scores = jnp.where(visible[None], scores, -1e30)
    row_peak = jnp.max(scores, axis=-1, keepdims=True)
    probs = jnp.where(visible[None], jnp.exp(scores - row_peak), 0.0)
    total = jnp.sum(probs, axis=-1, keepdims=True)
    mixed_heads = jnp.einsum(
        "hqk,khd->qhd", probs.astype(jnp.bfloat16), all_values, preferred_element_type=jnp.float32
    ) / jnp.transpose(total, (1, 0, 2))
    attended = mixed_heads.astype(jnp.bfloat16).reshape(tok_group, query_heads * HD)
    out_rows = wo.astype(jnp.bfloat16)
    attn_part = jnp.dot(
        attended,
        lax.all_gather(out_rows, "group", axis=1, tiled=True),
        preferred_element_type=jnp.float32,
    )
    mixed = residual + lax.psum(attn_part.astype(jnp.bfloat16), "tensor").astype(jnp.float32)
    normed_mlp = rms_scale(mixed, mlp_gain)
    gate_rows = w_gate.astype(jnp.bfloat16)
    up_rows = w_up.astype(jnp.bfloat16)
    gate_sum, up_sum = contract_rows(
        normed_mlp,
        (
            lax.all_gather(gate_rows, "group", axis=0, tiled=True),
            lax.all_gather(up_rows, "group", axis=0, tiled=True),
        ),
    )
    activation = (jax.nn.silu(gate_sum) * up_sum).astype(jnp.bfloat16)
    down_rows = w_down.astype(jnp.bfloat16)
    down_part = jnp.dot(
        activation,
        lax.all_gather(down_rows, "group", axis=1, tiled=True),
        preferred_element_type=jnp.float32,
    )
    summed = lax.psum(down_part.astype(jnp.bfloat16), "tensor").astype(jnp.float32)
    first_row = lax.axis_index("tensor") * rows_dev
    own_mixed = lax.dynamic_slice_in_dim(mixed, first_row, rows_dev, 0)
    own_summed = lax.dynamic_slice_in_dim(summed, first_row, rows_dev, 0)
    layer_out = (own_mixed + own_summed).astype(jnp.bfloat16)
    pages = page_table.shape[1]
    changed = jnp.concatenate(
        [jnp.ones((1,), jnp.int32), (request_of[1:] != request_of[:-1]).astype(jnp.int32)]
    )
    opens = jnp.maximum(changed, (positions % PAGE == 0).astype(jnp.int32))
    logical = jnp.cumsum(opens) - 1
    chosen = jnp.sum(
        jnp.where(logical[:, None] == jnp.arange(pages)[None, :], page_table, 0), axis=1
    )
    target = chosen * PAGE + positions % PAGE
    width = 2 * KVH * HD // tensor_count
    flat_rows = kv_rows.reshape(tok_group, key_heads * 2 * HD)
    offset = lax.axis_index("tensor") * width % (key_heads * 2 * HD)
    own_slice = lax.dynamic_slice_in_dim(flat_rows, offset, width, 1)
    cache = jnp.zeros((pages * PAGE, width), jnp.bfloat16).at[target].set(own_slice)
    return (layer_out, cache.reshape(pages, PAGE, width))


def solution(mesh):
    placed = (
        P(("group", "tensor"), None),
        P("group"),
        P("group"),
        P("group", None),
        P(),
        P(),
        P("group", "tensor"),
        P("group", "tensor"),
        P("group", "tensor"),
        P("tensor", "group"),
        P("group", "tensor"),
        P("group", "tensor"),
        P("tensor", "group"),
    )
    return jax.shard_map(
        body,
        mesh=mesh,
        in_specs=placed,
        out_specs=(P(("group", "tensor"), None), P("group", None, "tensor")),
        check_vma=False,
    )
```

profile of v0, /device:TPU:0, one launch (start us, length us, event | category | flops | bytes accessed | tf_op | source)
XLA Modules:
  0.0 593.4 jit_solution(9900236413319749413)
XLA Ops:
  8.0 0.0 copy-start.8
  8.0 0.0 all-gather.5.cloned.1.call-start
  8.1 0.7 all-gather.5.cloned.1.call-update
  8.8 0.0 all-reduce.3.cloned.1.call-start
  8.8 0.8 convert_element_type.103
  9.6 0.8 convert_element_type.108
  10.5 0.5 collective-permute-start.1
  11.0 0.9 convert_element_type.110
  11.9 1.2 slice.43
  13.1 1.2 slice.42
  14.3 0.8 slice_compare_fusion
  15.2 0.8 maximum_bitcast_fusion
  15.9 0.3 reduce-window.9
  16.2 0.1 slice.57
  16.3 0.9 convert_element_type.117
  17.9 0.1 slice_reduce_fusion
  18.0 0.1 add_bitcast_fusion
  18.1 0.8 select_reduce_fusion
  18.9 1.4 iota_compare_fusion.1
  20.2 0.8 compare_select_fusion
  21.0 30.5 %all_gather.27 = bf16[2048,128]{1,0:T(8,128)(2,1)S(1)} all-gather(bf16[256,128]{1,0:T(8,128)(2,1)S(1)} %convert_element_type.110), channel_id=1, replica_groups=mesh['group'=8,'tensor'=16] {'group'}, dimensions={0}, use_global_device_ids=true | all-gather | bytes 589824 | tf_op jit(solution)/shard_map/all_gather | solution.py:88
  51.6 32.5 %all_gather.28 = bf16[128,2048]{1,0:T(8,128)(2,1)} all-gather(bf16[128,256]{1,0:T(8,128)(2,1)S(1)} %convert_element_type.117), channel_id=1, replica_groups=mesh['group'=8,'tensor'=16] {'group'}, dimensions={1}, use_global_device_ids=true | all-gather | bytes 589824 | tf_op jit(solution)/shard_map/all_gather | solution.py:128
  84.0 3.3 compare_and_fusion
  87.5 29.4 %all_gather.25 = bf16[2048,128]{0,1:T(8,128)(2,1)S(1)} all-gather(bf16[256,128]{0,1:T(8,128)(2,1)S(1)} %pad_maximum_fusion.1), channel_id=1, replica_groups=mesh['group'=8,'tensor'=16] {'group'}, dimensions={0}, use_global_device_ids=true | all-gather | bytes 589824 | tf_op jit(solution)/shard_map/all_gather | solution.py:89
  116.8 30.9 %all_gather.26 = bf16[2048,128]{0,1:T(8,128)(2,1)} all-gather(bf16[256,128]{0,1:T(8,128)(2,1)S(1)} %pad_maximum_fusion.2), channel_id=1, replica_groups=mesh['group'=8,'tensor'=16] {'group'}, dimensions={0}, use_global_device_ids=true | all-gather | bytes 589824 | tf_op jit(solution)/shard_map/all_gather | solution.py:90
  147.7 4.2 fusion.1
  152.0 0.3 copy-done
  152.3 1.5 fusion.3
  153.8 2.2 fusion.13
  156.0 2.2 fusion.16
  158.3 2.2 fusion.14
  160.5 1.7 fusion.52
  162.2 0.1 pad_maximum_fusion
  162.3 4.2 collective-permute-start.2
  166.5 1.5 broadcast_and_fusion
  168.1 7.7 %collective-permute-done.2 = bf16[1536,1,2,128]{0,3,2,1:T(8,128)(2,1)S(1)} collective-permute-done((bf16[1536,1,2,128]{0,3,2,1:T(8,128)(2,1)S(1)}, bf16[1536,1,2,128]{0,3,2,1:T(8,128)(2,1)S(1)}, u32[]{:S(2)}, u32[]{:S(2)}) %collective-permute-start.2) | collective-permute-done | bytes 786464 | tf_op jit(solution)/shard_map/ppermute | solution.py:23
  175.8 0.2 maximum_maximum_fusion
  176.0 0.0 copy-start.3
  176.0 4.1 fusion
  180.1 6.4 %copy-done.1 = f32[1536,3072]{1,0:T(8,128)} copy-done((f32[1536,3072]{1,0:T(8,128)}, f32[1536,3072]{1,0:T(8,128)S(1)}, u32[]{:S(2)}) %copy-start.1) | copy-done | bytes 18874392
  186.5 6.4 %fusion.4 = f32[1536]{0:T(1024)S(1)} fusion(f32[1536,3072]{1,0:T(8,128)S(1)} %get-tuple-element.17, f32[1536]{0:T(1024)S(1)} %get-tuple-element.16, pred[1536,1536]{1,0:T(32,128)(4,1)S(1)} %compare_and_fusion, pred[1536,1536]{1,0:T(32,128)(4,1)S(1)} %broadcast_and_fusion), kind=kLoop, calls=%fused_computation.13 | loop fusion | flops 28310016 | bytes 23605248 | tf_op jit(solution)/shard_map/reduce_sum | solution.py:120
  192.9 14.1 %convolution_convert_fusion.1 = bf16[1536,2048]{1,0:T(8,128)(2,1)} fusion(bf16[128,2048]{1,0:T(8,128)(2,1)} %all_gather.28, f32[1536,3072]{1,0:T(8,128)} %copy-done.1, f32[1536]{0:T(1024)S(1)} %get-tuple-element.16, bf16[3072,1,2,128]{0,3,2,1:T(8,128)(2,1)} %copy-done.3, f32[1536]{0:T(1024)S(1)} %fusion.4, pred[1536,1536]{1,0:T(32,128)(4,1)S(1)} %compare_and_fusion, ...), kind=kOutput, calls=%fused_computation.18 | convolution fusion | flops 2045116416 | bytes 31207424 | tf_op jit(solution)/shard_map/dot_general | solution.py:126
  207.0 0.0 all-reduce.3.cloned.1.call-update
  207.1 0.0 all-gather.7.cloned.1.call-start
  207.1 1.0 copy-done.4
  208.1 0.8 convert_element_type.121
  208.8 0.0 all-gather.7.cloned.1.call-update
  208.8 0.0 all-gather.11.cloned.1.call-start
  208.9 0.7 convert_element_type.124
  209.6 0.0 all-gather.11.cloned.1.call-update
  209.7 0.0 all-gather.9.cloned.1.call-start
  209.7 0.7 convert_element_type.122
  210.5 0.0 all-gather.9.cloned.1.call-update
  210.5 0.0 copy-start.11
  210.5 0.3 all-reduce.5.cloned.1.call-start
  210.8 179.3 %all-reduce.3.cloned.1.call-done = bf16[1536,2048]{1,0:T(8,128)(2,1)} async-done(((bf16[1536,2048]{1,0:T(8,128)(2,1)}), bf16[1536,2048]{1,0:T(8,128)(2,1)}) %all-reduce.3.cloned.1.call-update) | async-done | bytes 6291472 | tf_op jit(solution)/shard_map/psum | solution.py:131
  390.1 11.2 %multiply_reduce_fusion = (f32[1536]{0:T(1024)S(1)}, f32[1536,2048]{1,0:T(8,128)}) fusion(bf16[1536,2048]{1,0:T(8,128)(2,1)} %all-reduce.3.cloned.1.call-done, bf16[1536,2048]{1,0:T(8,128)(2,1)} %all-gather.5.cloned.1.call-done), kind=kLoop, calls=%fused_computation.12 | loop fusion | flops 15727104 | bytes 25171968 | tf_op jit(solution)/shard_map/reduce_sum | solution.py:27
  401.3 10.4 %fusion.64 = f32[1536,512]{1,0:T(8,128)} fusion(bf16[2048,512]{1,0:T(8,128)(2,1)} %all-gather.7.cloned.1.call-done, f32[2048]{0:T(1024)S(1)} %copy-done.11, f32[1536]{0:T(1024)S(1)} %add_rsqrt_fusion, bf16[1536,2048]{1,0:T(8,128)(2,1)} %all-gather.5.cloned.1.call-done, bf16[1536,2048]{1,0:T(8,128)(2,1)} %all-reduce.3.cloned.1.call-done), kind=kOutput, calls=%fused_computation.96 | convolution fusion | flops 3240099840 | bytes 17840128 | tf_op jit(solution)/shard_map/dot_general | solution.py:53
  411.7 15.3 %convolution_convert_fusion = bf16[1536,2048]{1,0:T(8,128)(2,1)} fusion(bf16[512,2048]{1,0:T(8,128)(2,1)} %all-gather.11.cloned.1.call-done, bf16[2048,512]{1,0:T(8,128)(2,1)} %all-gather.9.cloned.1.call-done, f32[1536,512]{1,0:T(8,128)} %fusion.64, f32[2048]{0:T(1024)S(1)} %copy-done.11, f32[1536]{0:T(1024)S(1)} %add_rsqrt_fusion, ...), kind=kOutput, calls=%fused_computation.17 | convolution fusion | flops 6469189632 | bytes 26228736 | tf_op jit(solution)/shard_map/dot_general | solution.py:144
  427.0 0.0 all-reduce.5.cloned.1.call-update
  427.1 0.2 copy.17
  427.3 6.1 %scatter_custom_fusion = bf16[8192,128]{1,0:T(8,128)(2,1)} fusion(s32[1536]{0:T(1024)S(1)} %get-tuple-element.14, bf16[1536,128]{1,0:T(8,128)(2,1)S(1)} %copy.17, bf16[]{:T(256)} %constant.84.clone.1), kind=kCustom, calls=%fused_computation.35 | custom fusion | bytes 2097154 | tf_op jit(solution)/shard_map/scatter | solution.py:168
  433.4 150.6 %all-reduce.5.cloned.1.call-done = bf16[1536,2048]{1,0:T(8,128)(2,1)} async-done(((bf16[1536,2048]{1,0:T(8,128)(2,1)}), bf16[1536,2048]{1,0:T(8,128)(2,1)}) %all-reduce.5.cloned.1.call-update) | async-done | bytes 6291472 | tf_op jit(solution)/shard_map/psum | solution.py:149
  584.0 2.1 add_convert_fusion
  (33 shorter events, 0.2 us)
Async XLA Ops:
  8.0 79.4 %copy-start.9 = (f32[256,64]{0,1:T(8,128)S(1)}, f32[256,64]{0,1:T(8,128)}, u32[]{:S(2)}) copy-start(f32[256,64]{0,1:T(8,128)} %param.20) | copy-start | bytes 196612
  8.0 79.4 %copy-start.8 = (f32[256,64]{0,1:T(8,128)S(1)}, f32[256,64]{0,1:T(8,128)}, u32[]{:S(2)}) copy-start(f32[256,64]{0,1:T(8,128)} %param.21) | copy-start | bytes 196612
  8.0 139.7 %all-gather.5.cloned.1.call-start = ((), (), s32[]{:S(2)}) async-start(), calls=%async_computation | async-start | bytes 6684672 | tf_op jit(solution)/shard_map/all_gather | solution.py:77
  8.8 381.3 %all-reduce.3.cloned.1.call-start = ((), (), s32[]{:S(2)}) async-start(), calls=%async_computation.1 | async-start | bytes 12582912 | tf_op jit(solution)/shard_map/psum | solution.py:131
  9.6 77.7 %collective-permute-start = (bf16[256,64]{0,1:T(8,128)(2,1)S(1)}, bf16[256,64]{0,1:T(8,128)(2,1)S(1)}, u32[]{:S(2)}, u32[]{:S(2)}) collective-permute-start(bf16[256,64]{0,1:T(8,128)(2,1)S(1)} %convert_element_type.103), channel_id=1, source_target_pairs={{0,1},{1,0},{2,3},{3,2},{4,5},{5,4},{6,7},{7,6},{8,9},{9,8},{10,11... | collective-permute-start | bytes 98312 | tf_op jit(solution)/shard_map/ppermute | solution.py:17
  10.5 76.9 %collective-permute-start.1 = (bf16[256,64]{0,1:T(8,128)(2,1)S(1)}, bf16[256,64]{0,1:T(8,128)(2,1)S(1)}, u32[]{:S(2)}, u32[]{:S(2)}) collective-permute-start(bf16[256,64]{0,1:T(8,128)(2,1)S(1)} %convert_element_type.108), channel_id=1, source_target_pairs={{0,1},{1,0},{2,3},{3,2},{4,5},{5,4},{6,7},{7,6},{8,9},{9,8},{10,11... | collective-permute-start | bytes 98312 | tf_op jit(solution)/shard_map/ppermute | solution.py:17
  84.0 67.9 %copy-start.10 = (f32[2048]{0:T(1024)S(1)}, f32[2048]{0:T(1024)}, u32[]{:S(2)}) copy-start(f32[2048]{0:T(1024)} %param.17) | copy-start | bytes 24580
  147.7 4.6 copy-start
  156.0 2.2 copy-start.7
  162.3 13.5 %collective-permute-start.2 = (bf16[1536,1,2,128]{0,3,2,1:T(8,128)(2,1)S(1)}, bf16[1536,1,2,128]{0,3,2,1:T(8,128)(2,1)S(1)}, u32[]{:S(2)}, u32[]{:S(2)}) collective-permute-start(bf16[1536,1,2,128]{0,3,2,1:T(8,128)(2,1)S(1)} %pad_maximum_fusion), channel_id=1, source_target_pairs={{0,16},{16,32},{32,48},{48,64},{64,80},{80,96},{96,112},{1,17},{17... | collective-permute-start | bytes 2359304 | tf_op jit(solution)/shard_map/ppermute | solution.py:23
  168.1 12.0 %copy-start.2 = (pred[1536,1536]{1,0:T(32,128)(4,1)}, pred[1536,1536]{1,0:T(32,128)(4,1)S(1)}, u32[]{:S(2)}) copy-start(pred[1536,1536]{1,0:T(32,128)(4,1)S(1)} %broadcast_and_fusion) | copy-start | bytes 7077892
  176.0 4.1 copy-start.3
  180.1 6.5 %copy-start.1 = (f32[1536,3072]{1,0:T(8,128)}, f32[1536,3072]{1,0:T(8,128)S(1)}, u32[]{:S(2)}) copy-start(f32[1536,3072]{1,0:T(8,128)S(1)} %get-tuple-element.17) | copy-start | bytes 56623108
  207.0 1.0 copy-start.4
  207.0 1.9 copy-start.5
  207.0 2.7 copy-start.6
  207.1 194.2 %all-gather.7.cloned.1.call-start = ((), (), s32[]{:S(2)}) async-start(), calls=%async_computation.2 | async-start | bytes 2359296 | tf_op jit(solution)/shard_map/all_gather | solution.py:138
  208.8 202.8 %all-gather.11.cloned.1.call-start = ((), (), s32[]{:S(2)}) async-start(), calls=%async_computation.4 | async-start | bytes 2359296 | tf_op jit(solution)/shard_map/all_gather | solution.py:146
  209.7 202.0 %all-gather.9.cloned.1.call-start = ((), (), s32[]{:S(2)}) async-start(), calls=%async_computation.3 | async-start | bytes 2359296 | tf_op jit(solution)/shard_map/all_gather | solution.py:139
  210.5 190.8 %copy-start.11 = (f32[2048]{0:T(1024)S(1)}, f32[2048]{0:T(1024)}, u32[]{:S(2)}) copy-start(f32[2048]{0:T(1024)} %param.18) | copy-start | bytes 24580
  210.5 373.5 %all-reduce.5.cloned.1.call-start = ((), (), s32[]{:S(2)}) async-start(), calls=%async_computation.5 | async-start | bytes 12582912 | tf_op jit(solution)/shard_map/psum | solution.py:149
Sparse Core Ops, SparseCore 0:
  11.3 70.2 all-gather.4
  207.2 182.8 all-reduce.2
  427.1 156.8 all-reduce.4
Sparse Core Ops, SparseCore 1:
  209.2 49.1 all-gather.6
  260.3 41.6 all-gather.10
  304.1 50.6 all-gather.8
where the time goes:
time: 594 us; the launch traced here: 593 us
  waiting for transfers between devices  338 us (57%)
  blocking collectives  123 us (21%)
  matrix products  50.5 us (9%)
  other arithmetic  42.9 us (7%)
  local copies, waits for them, and re-layouts  16.7 us (3%)
  between operations  16.4 us (3%)
    psum x1, waiting for transfers between devices, body(): lax.psum(attn_part.astype(jnp.bfloat16), 'tensor').astype(jnp.float32)  179 us
    psum x1, waiting for transfers between devices, body(): lax.psum(down_part.astype(jnp.bfloat16), 'tensor').astype(jnp.float32)  151 us
    all_gather x1, blocking collectives, body(): lax.all_gather(out_rows, 'group', axis=1, tiled=True)  32.5 us
    all_gather x1, blocking collectives, body(): lax.all_gather(value_rows, 'group', axis=0, tiled=True)  30.9 us
    all_gather x1, blocking collectives, body(): lax.all_gather(query_rows, 'group', axis=0, tiled=True)  30.5 us
    all_gather x1, blocking collectives, body(): lax.all_gather(key_rows, 'group', axis=0, tiled=True)  29.4 us
    dot_general x4, matrix products, contract_rows(): jnp.dot(acts, piece, preferred_element_type=jnp.float32)  17 us
    reduce_sum x2, other arithmetic, rms_scale(): square = jnp.mean(values * values, axis=-1, keepdims=True)  15.4 us
  transfers between devices with their start and end apart: 9, of which 3 were waited for; matrix products, arithmetic and copies ran while one was open for 8% of the time, Pallas kernels for 0%

commit v1 on v0

--- a/solution.py
+++ b/solution.py
@@ -1,3 +1,4 @@
+import functools
 import jax
 import jax.numpy as jnp
 from jax import lax
@@ -9,6 +10,14 @@
 PAGE = 128
 rope_base = 1000000.0
 norm_eps = 1e-06
+
+
+def carry_the_sides(unit, net_axis):
+    t_next = lax.all_gather(unit, axis_name=net_axis).sum(axis=0)
+    return t_next
+
+
+start_case = functools.partial(carry_the_sides, net_axis="tensor")
 
 
 def partner(value, axis, distance):
@@ -128,7 +137,7 @@
         lax.all_gather(out_rows, "group", axis=1, tiled=True),
         preferred_element_type=jnp.float32,
     )
-    mixed = residual + lax.psum(attn_part.astype(jnp.bfloat16), "tensor").astype(jnp.float32)
+    mixed = residual + start_case(attn_part.astype(jnp.bfloat16)).astype(jnp.float32)
     normed_mlp = rms_scale(mixed, mlp_gain)
     gate_rows = w_gate.astype(jnp.bfloat16)
     up_rows = w_up.astype(jnp.bfloat16)

time: 594 us -> 1020 us (1.72)
  waiting for transfers between devices: 338 us -> 725 us
  other arithmetic: 42.9 us -> 77.9 us
    all_gather x0 -> x1, waiting for transfers between devices: none -> 491 us  [carry_the_sides(): t_next = lax.all_gather(unit, axis_name=net_axis).sum(axis=0)]
    psum x1 -> x0, waiting for transfers between devices: 179 us -> none  [body(): lax.psum(attn_part.astype(jnp.bfloat16), 'tensor').astype(jnp.float32)]
    all_gather x1, waiting for transfers between devices: 0.01 us -> 46.2 us  [body(): lax.all_gather(down_rows, 'group', axis=1, tiled=True)]
    reduce_sum x0 -> x1, other arithmetic: none -> 35.1 us  [carry_the_sides(): t_next = lax.all_gather(unit, axis_name=net_axis).sum(axis=0)]
    all_gather x1, waiting for transfers between devices: 0.01 us -> 27.1 us  [body(): lax.all_gather(up_rows, 'group', axis=0, tiled=True)]
  transfers between devices with their start and end apart: 9 -> 9, of which waited for: 3 -> 5; matrix products, arithmetic and copies ran while one was open for 8% -> 8% of each run, Pallas kernels for 0% -> 0%
where the time goes in v1:
time: 1020 us; the launch traced here: 1010 us
  waiting for transfers between devices  725 us (71%)
  blocking collectives  123 us (12%)
  other arithmetic  77.9 us (8%)
  matrix products  50.6 us (5%)
  local copies, waits for them, and re-layouts  16.8 us (2%)
  between operations  15.5 us (2%)
    all_gather x1, waiting for transfers between devices, carry_the_sides(): t_next = lax.all_gather(unit, axis_name=net_axis).sum(axis=0)  491 us
    psum x1, waiting for transfers between devices, body(): lax.psum(down_part.astype(jnp.bfloat16), 'tensor').astype(jnp.float32)  152 us
    all_gather x1, waiting for transfers between devices, body(): lax.all_gather(down_rows, 'group', axis=1, tiled=True)  46.2 us
    reduce_sum x1, other arithmetic, carry_the_sides(): t_next = lax.all_gather(unit, axis_name=net_axis).sum(axis=0)  35.1 us
    all_gather x1, blocking collectives, body(): lax.all_gather(out_rows, 'group', axis=1, tiled=True)  32.5 us
    all_gather x1, blocking collectives, body(): lax.all_gather(value_rows, 'group', axis=0, tiled=True)  30.9 us
    all_gather x1, blocking collectives, body(): lax.all_gather(query_rows, 'group', axis=0, tiled=True)  30.5 us
    all_gather x1, blocking collectives, body(): lax.all_gather(key_rows, 'group', axis=0, tiled=True)  29.4 us
  transfers between devices with their start and end apart: 9, of which 5 were waited for; matrix products, arithmetic and copies ran while one was open for 8% of the time, Pallas kernels for 0%

profile of v1, /device:TPU:0, one launch (start us, length us, event | category | flops | bytes accessed | tf_op | source)
XLA Modules:
  0.0 1014.2 jit_solution(1188733496348914486)
XLA Ops:
  7.2 0.0 all-gather.7.cloned.1.call-start
  7.2 0.7 all-gather.7.cloned.1.call-update
  7.9 0.0 all-gather.15.cloned.1.call-start
  8.0 0.8 convert_element_type.105
  8.8 0.8 convert_element_type.110
  9.7 0.5 collective-permute-start.1
  10.2 0.9 convert_element_type.112
  11.1 1.2 slice.43
  12.3 1.2 slice.42
  13.5 0.8 slice_compare_fusion
  14.3 0.8 maximum_bitcast_fusion
  15.1 0.3 reduce-window.9
  15.4 0.1 slice.57
  15.5 0.9 convert_element_type.119
  17.1 0.1 slice_reduce_fusion
  17.2 0.1 add_bitcast_fusion
  17.2 0.8 select_reduce_fusion
  18.0 1.4 iota_compare_fusion.1
  19.4 0.8 compare_select_fusion
  20.2 30.5 %all_gather.33 = bf16[2048,128]{1,0:T(8,128)(2,1)S(1)} all-gather(bf16[256,128]{1,0:T(8,128)(2,1)S(1)} %convert_element_type.112), channel_id=1, replica_groups=mesh['group'=8,'tensor'=16] {'group'}, dimensions={0}, use_global_device_ids=true | all-gather | bytes 589824 | tf_op jit(solution)/shard_map/all_gather | solution.py:97
  50.7 32.5 %all_gather.34 = bf16[128,2048]{1,0:T(8,128)(2,1)} all-gather(bf16[128,256]{1,0:T(8,128)(2,1)S(1)} %convert_element_type.119), channel_id=1, replica_groups=mesh['group'=8,'tensor'=16] {'group'}, dimensions={1}, use_global_device_ids=true | all-gather | bytes 589824 | tf_op jit(solution)/shard_map/all_gather | solution.py:137
  83.2 3.3 compare_and_fusion
  86.7 29.4 %all_gather.31 = bf16[2048,128]{0,1:T(8,128)(2,1)S(1)} all-gather(bf16[256,128]{0,1:T(8,128)(2,1)S(1)} %pad_maximum_fusion.1), channel_id=1, replica_groups=mesh['group'=8,'tensor'=16] {'group'}, dimensions={0}, use_global_device_ids=true | all-gather | bytes 589824 | tf_op jit(solution)/shard_map/all_gather | solution.py:98
  116.0 30.9 %all_gather.32 = bf16[2048,128]{0,1:T(8,128)(2,1)} all-gather(bf16[256,128]{0,1:T(8,128)(2,1)S(1)} %pad_maximum_fusion.2), channel_id=1, replica_groups=mesh['group'=8,'tensor'=16] {'group'}, dimensions={0}, use_global_device_ids=true | all-gather | bytes 589824 | tf_op jit(solution)/shard_map/all_gather | solution.py:99
  146.9 4.2 fusion.1
  151.1 0.3 copy-done
  151.5 1.5 fusion.3
  153.0 2.2 fusion.13
  155.2 2.2 fusion.16
  157.4 2.2 fusion.14
  159.6 1.7 fusion.52
  161.4 0.1 pad_maximum_fusion
  161.5 4.2 collective-permute-start.2
  165.7 1.5 broadcast_and_fusion
  167.3 7.7 collective-permute-done.2
  175.0 0.2 maximum_maximum_fusion
  175.1 4.1 fusion
  179.3 6.4 copy-done.1
  185.7 6.4 fusion.4
  192.1 14.2 %convolution_convert_fusion.1 = bf16[1536,2048]{1,0:T(8,128)(2,1)} fusion(bf16[128,2048]{1,0:T(8,128)(2,1)} %all_gather.34, f32[1536,3072]{1,0:T(8,128)} %copy-done.1, f32[1536]{0:T(1024)S(1)} %get-tuple-element.16, bf16[3072,1,2,128]{0,3,2,1:T(8,128)(2,1)} %copy-done.3, f32[1536]{0:T(1024)S(1)} %fusion.4, pred[1536,1536]{1,0:T(32,128)(4,1)S(1)} %compare_and_fusion, ...), kind=kOutput, calls=%fused_computation.18 | convolution fusion | flops 2045116416 | bytes 31207424 | tf_op jit(solution)/shard_map/dot_general | solution.py:135
  206.3 0.0 all-gather.15.cloned.1.call-update
  206.3 0.0 all-gather.9.cloned.1.call-start
  206.3 1.0 copy-done.4
  207.3 0.7 convert_element_type.123
  208.0 0.0 all-gather.9.cloned.1.call-update
  208.1 0.0 all-gather.11.cloned.1.call-start
  208.1 0.7 convert_element_type.124
  208.9 0.0 all-gather.11.cloned.1.call-update
  208.9 0.0 all-gather.13.cloned.1.call-start
  209.0 0.7 convert_element_type.126
  209.7 0.0 all-gather.13.cloned.1.call-update
  209.7 0.0 all-reduce.2.cloned.1.call-start
  209.8 491.4 %all-gather.15.cloned.1.call-done = bf16[24576,2048]{1,0:T(8,128)(2,1)} async-done(((bf16[1536,2048]{1,0:T(8,128)(2,1)}), bf16[24576,2048]{1,0:T(8,128)(2,1)}) %all-gather.15.cloned.1.call-update) | async-done | bytes 100663312 | tf_op jit(solution)/shard_map/all_gather | solution.py:16
  701.1 35.1 %reduce_sum.50 = bf16[1536,2048]{1,0:T(8,128)(2,1)} reduce(bf16[16,1536,2048]{2,1,0:T(8,128)(2,1)} %bitcast.16, bf16[]{:T(256)} %constant.82.clone.1), dimensions={0}, to_apply=%region_3.4 | reduce | flops 47185920 | bytes 106954752 | tf_op jit(solution)/shard_map/reduce_sum | solution.py:16
  736.2 11.2 %multiply_reduce_fusion = (f32[1536]{0:T(1024)S(1)}, f32[1536,2048]{1,0:T(8,128)}) fusion(bf16[1536,2048]{1,0:T(8,128)(2,1)} %reduce_sum.50, bf16[1536,2048]{1,0:T(8,128)(2,1)} %all-gather.7.cloned.1.call-done), kind=kLoop, calls=%fused_computation.12 | loop fusion | flops 15727104 | bytes 25171968 | tf_op jit(solution)/shard_map/reduce_sum | solution.py:36
  747.4 10.5 %fusion.64 = f32[1536,512]{1,0:T(8,128)} fusion(bf16[2048,512]{1,0:T(8,128)(2,1)} %all-gather.9.cloned.1.call-done, f32[2048]{0:T(1024)S(1)} %copy-done.11, f32[1536]{0:T(1024)S(1)} %add_rsqrt_fusion, bf16[1536,2048]{1,0:T(8,128)(2,1)} %all-gather.7.cloned.1.call-done, bf16[1536,2048]{1,0:T(8,128)(2,1)} %reduce_sum.50), kind=kOutput, calls=%fused_computation.96 | convolution fusion | flops 3240099840 | bytes 17840128 | tf_op jit(solution)/shard_map/dot_general | solution.py:62
  757.9 27.1 %all-gather.11.cloned.1.call-done = bf16[2048,512]{1,0:T(8,128)(2,1)} async-done(((bf16[256,512]{1,0:T(8,128)(2,1)}), bf16[2048,512]{1,0:T(8,128)(2,1)}) %all-gather.11.cloned.1.call-update) | async-done | bytes 2097168 | tf_op jit(solution)/shard_map/all_gather | solution.py:148
  784.9 46.2 %all-gather.13.cloned.1.call-done = bf16[512,2048]{1,0:T(8,128)(2,1)} async-done(((bf16[512,256]{1,0:T(8,128)(2,1)}), bf16[512,2048]{1,0:T(8,128)(2,1)}) %all-gather.13.cloned.1.call-update) | async-done | bytes 2097168 | tf_op jit(solution)/shard_map/all_gather | solution.py:155
  831.2 15.3 %convolution_convert_fusion = bf16[1536,2048]{1,0:T(8,128)(2,1)} fusion(bf16[512,2048]{1,0:T(8,128)(2,1)} %all-gather.13.cloned.1.call-done, bf16[2048,512]{1,0:T(8,128)(2,1)} %all-gather.11.cloned.1.call-done, f32[1536,512]{1,0:T(8,128)} %fusion.64, f32[2048]{0:T(1024)S(1)} %copy-done.11, f32[1536]{0:T(1024)S(1)} %add_rsqrt_fusion, ...), kind=kOutput, calls=%fused_computation.17 | convolution fusion | flops 6469189632 | bytes 26228736 | tf_op jit(solution)/shard_map/dot_general | solution.py:153
  846.5 0.0 all-reduce.2.cloned.1.call-update
  846.6 0.2 copy.17
  846.8 6.1 scatter_custom_fusion
  852.9 152.0 %all-reduce.2.cloned.1.call-done = bf16[1536,2048]{1,0:T(8,128)(2,1)} async-done(((bf16[1536,2048]{1,0:T(8,128)(2,1)}), bf16[1536,2048]{1,0:T(8,128)(2,1)}) %all-reduce.2.cloned.1.call-update) | async-done | bytes 6291472 | tf_op jit(solution)/shard_map/psum | solution.py:158
  1004.9 2.1 add_convert_fusion
  (34 shorter events, 0.2 us)
Async XLA Ops:
  7.2 79.4 %copy-start.9 = (f32[256,64]{0,1:T(8,128)S(1)}, f32[256,64]{0,1:T(8,128)}, u32[]{:S(2)}) copy-start(f32[256,64]{0,1:T(8,128)} %param.20) | copy-start | bytes 196612
  7.2 79.4 %copy-start.8 = (f32[256,64]{0,1:T(8,128)S(1)}, f32[256,64]{0,1:T(8,128)}, u32[]{:S(2)}) copy-start(f32[256,64]{0,1:T(8,128)} %param.21) | copy-start | bytes 196612
  7.2 139.7 %all-gather.7.cloned.1.call-start = ((), (), s32[]{:S(2)}) async-start(), calls=%async_computation | async-start | bytes 6684672 | tf_op jit(solution)/shard_map/all_gather | solution.py:86
  7.9 693.2 %all-gather.15.cloned.1.call-start = ((), (), s32[]{:S(2)}) async-start(), calls=%async_computation.5 | async-start | bytes 106954752 | tf_op jit(solution)/shard_map/all_gather | solution.py:16
  8.8 77.7 %collective-permute-start = (bf16[256,64]{0,1:T(8,128)(2,1)S(1)}, bf16[256,64]{0,1:T(8,128)(2,1)S(1)}, u32[]{:S(2)}, u32[]{:S(2)}) collective-permute-start(bf16[256,64]{0,1:T(8,128)(2,1)S(1)} %convert_element_type.105), channel_id=1, source_target_pairs={{0,1},{1,0},{2,3},{3,2},{4,5},{5,4},{6,7},{7,6},{8,9},{9,8},{10,11... | collective-permute-start | bytes 98312 | tf_op jit(solution)/shard_map/ppermute | solution.py:26
  9.7 76.9 %collective-permute-start.1 = (bf16[256,64]{0,1:T(8,128)(2,1)S(1)}, bf16[256,64]{0,1:T(8,128)(2,1)S(1)}, u32[]{:S(2)}, u32[]{:S(2)}) collective-permute-start(bf16[256,64]{0,1:T(8,128)(2,1)S(1)} %convert_element_type.110), channel_id=1, source_target_pairs={{0,1},{1,0},{2,3},{3,2},{4,5},{5,4},{6,7},{7,6},{8,9},{9,8},{10,11... | collective-permute-start | bytes 98312 | tf_op jit(solution)/shard_map/ppermute | solution.py:26
  83.2 67.9 %copy-start.10 = (f32[2048]{0:T(1024)S(1)}, f32[2048]{0:T(1024)}, u32[]{:S(2)}) copy-start(f32[2048]{0:T(1024)} %param.17) | copy-start | bytes 24580
  146.9 4.6 copy-start
  155.2 2.2 copy-start.7
  161.5 13.5 %collective-permute-start.2 = (bf16[1536,1,2,128]{0,3,2,1:T(8,128)(2,1)S(1)}, bf16[1536,1,2,128]{0,3,2,1:T(8,128)(2,1)S(1)}, u32[]{:S(2)}, u32[]{:S(2)}) collective-permute-start(bf16[1536,1,2,128]{0,3,2,1:T(8,128)(2,1)S(1)} %pad_maximum_fusion), channel_id=1, source_target_pairs={{0,16},{16,32},{32,48},{48,64},{64,80},{80,96},{96,112},{1,17},{17... | collective-permute-start | bytes 2359304 | tf_op jit(solution)/shard_map/ppermute | solution.py:32
  167.2 12.0 %copy-start.2 = (pred[1536,1536]{1,0:T(32,128)(4,1)}, pred[1536,1536]{1,0:T(32,128)(4,1)S(1)}, u32[]{:S(2)}) copy-start(pred[1536,1536]{1,0:T(32,128)(4,1)S(1)} %broadcast_and_fusion) | copy-start | bytes 7077892
  175.1 4.1 copy-start.3
  179.2 6.5 copy-start.1
  206.3 1.0 copy-start.4
  206.3 1.9 copy-start.5
  206.3 2.7 copy-start.6
  206.3 541.1 %all-gather.9.cloned.1.call-start = ((), (), s32[]{:S(2)}) async-start(), calls=%async_computation.1 | async-start | bytes 2359296 | tf_op jit(solution)/shard_map/all_gather | solution.py:147
  208.1 576.8 %all-gather.11.cloned.1.call-start = ((), (), s32[]{:S(2)}) async-start(), calls=%async_computation.2 | async-start | bytes 2359296 | tf_op jit(solution)/shard_map/all_gather | solution.py:148
  208.9 622.3 %all-gather.13.cloned.1.call-start = ((), (), s32[]{:S(2)}) async-start(), calls=%async_computation.3 | async-start | bytes 2359296 | tf_op jit(solution)/shard_map/all_gather | solution.py:155
  209.7 795.2 %all-reduce.2.cloned.1.call-start = ((), (), s32[]{:S(2)}) async-start(), calls=%async_computation.4 | async-start | bytes 12582912 | tf_op jit(solution)/shard_map/psum | solution.py:158
  736.2 11.2 %copy-start.11 = (f32[2048]{0:T(1024)S(1)}, f32[2048]{0:T(1024)}, u32[]{:S(2)}) copy-start(f32[2048]{0:T(1024)} %param.18) | copy-start | bytes 24580
Sparse Core Ops, SparseCore 0:
  10.5 70.2 all-gather.6
  206.4 494.6 all-gather.14
  702.8 39.1 all-gather.8
  744.0 40.8 all-gather.10
  786.9 44.2 all-gather.12
  846.6 158.2 all-reduce.1
